TPU v7x, 256 devices: a whole 4x4x8 slice. The times are simulated.
256 devices in a mesh: ctx: 32 (over y, x, core), head: 8 (over z).
Axes of the slice: x: 4, y: 4, z: 8, core: 2. Of those that a mesh axis runs over, the one named last changes fastest.
Arguments:
- queries: bfloat16 [8192, 4096], P('ctx', 'head'), may hold values from -168 to 168, as said below
- keys: bfloat16 [8192, 1024], P('ctx', 'head'), may hold values from -6.05 to 6.05, as said below
- values: bfloat16 [8192, 1024], P('ctx', 'head'), may hold values from -6 to 6
- d_y: bfloat16 [8192, 4096], P('ctx', 'head'), may hold values from -6 to 6
- w_out: bfloat16 [4096, 4096], P('head'), may hold values from -0.09375 to 0.09375
- key_blocks: int32 [64, 32], replicated, may hold values from 0 to 63, as said below
- block_count: int32 [64], replicated, may hold values from 1 to 32, as said below
Outputs:
- d_queries: bfloat16 [8192, 4096], P('ctx', 'head')
- keys_gradient: bfloat16 [8192, 1024], P('ctx', 'head')
- values_gradient: bfloat16 [8192, 1024], P('ctx', 'head')
Inputs may be any that keep to these rules, and one draw needn't show every extreme that they name: `key_blocks`: each row holds 32 distinct block numbers; its first block_count entries are at most the query block's own number, and the first entry is that number. Later entries are read by nobody. `block_count`: the last query block has 32 live entries; query block b has at most b // 2 + 1. `queries`: values stay within the bound. `keys`: values stay within the bound.
All inputs are finite; a program needn't handle non-finite values.
Results may differ from a plain program's by a relative error of at most 0.017.
Values may be sent and summed in bfloat16 or wider, within the bound.
No kernel may reach another device: no remote copies, remote signals or barrier semaphores. Data moves between devices by JAX's collectives and lax.ppermute only.
A program may use at most 64 MiB of HBM per device.

v0:
```python
import functools
import math

import jax
import jax.numpy as jnp
from jax import lax
from jax.experimental import pallas as pl
from jax.experimental.pallas import tpu as pltpu
from jax.sharding import Mesh
from jax.sharding import PartitionSpec as P

WIDTH = 128
SPAN = 128
HEADS = 4
ROWS = HEADS * SPAN
SCALE = 1.0 / math.sqrt(WIDTH)
LOG2E = 1.4426950408889634
NEG = -1e30
TILE = 4
PARTS = 4
CHIP_AXES = ("y", "x")
TOKEN_AXES = ("y", "x", "core")
NT = (((1,), (1,)), ((), ()))
TN = (((0,), (0,)), ((), ()))
f32 = jnp.float32
bf16 = jnp.bfloat16


def my_chip():
    return lax.axis_index("y") * lax.axis_size("x") + lax.axis_index("x")


def query_block(j, chip, core):
    side = jnp.where(j < 2, core, 1 - core)
    chips = lax.axis_size("y") * lax.axis_size("x")
    holder = jnp.where(side == 0, chip, chips - 1 - chip)
    return 4 * holder + 2 * side + j % 2


def head_block(j, h):
    return slice((j % 2) * SPAN, (j % 2 + 1) * SPAN), slice(h * WIDTH, (h + 1) * WIDTH)


def stack_heads(dst, own, sib):
    for j in range(4):
        src = own if j < 2 else sib
        for h in range(HEADS):
            dst[j, h * SPAN : (h + 1) * SPAN, :] = src[head_block(j, h)]


def head_copies(dst, own, sib, sems):
    copies = []
    for j in range(4):
        src = own if j < 2 else sib
        for h in range(HEADS):
            to = dst.at[j, h * SPAN : (h + 1) * SPAN, :]
            copies.append(
                pltpu.make_async_copy(src.at[head_block(j, h)], to, sems.at[j * HEADS + h])
            )
    return copies


def list_blocks(kb, bc, lst, b, core):
    def step(s, n):
        blk = kb[b, s]
        lst[n] = 4 * (blk // 4) + blk % 2
        return n + jnp.where((blk // 2) % 2 == core, 1, 0)

    n = lax.fori_loop(1, bc[b], step, 0)
    for t in range(TILE):
        lst[n + t] = 4 * (b // 4) + b % 2
    return n


def block_rows(i):
    return pl.ds(pl.multiple_of(i * SPAN, SPAN), SPAN)


def rows_of(ref, idxs):
    parts = [ref[block_rows(i), :] for i in idxs]
    return parts[0] if len(parts) == 1 else jnp.concatenate(parts, axis=0)


def hide(x, limits, fill):
    key = lax.broadcasted_iota(jnp.int32, (SPAN, ROWS), 0)
    qry = lax.broadcasted_iota(jnp.int32, (SPAN, ROWS), 1) % SPAN
    parts = [
        jnp.where(key - qry <= limit, x[t * SPAN : (t + 1) * SPAN], fill)
        for t, limit in enumerate(limits)
    ]
    return jnp.concatenate(parts, axis=0)


def walk(kb, bc, lst, b, core, visit, carry):
    n = list_blocks(kb, bc, lst, b, core)
    has_diag = jnp.where((b // 2) % 2 == core, 1, 0)
    tiles = n // TILE
    done = tiles * TILE
    rest = n - done
    left = rest + has_diag
    carry = lax.fori_loop(
        0, tiles, lambda t, c: visit(c, [lst[t * TILE + i] for i in range(TILE)], None), carry
    )

    def last(count):
        def run(c):
            limits = [
                jnp.where(t < rest, SPAN, jnp.where(t == rest, has_diag * 2 * SPAN, 0) - 2 * SPAN)
                for t in range(count)
            ]
            return visit(c, [lst[done + t] for t in range(count)], limits)

        return run

    def some(c):
        return lax.cond(left <= TILE // 2, last(TILE // 2), last(TILE), c)

    return lax.cond(left > 0, some, lambda c: c, carry)


def spread_kernel(keys, values, out, sems):
    chips, tok = out.shape[0], keys.shape[0]
    copies = []
    for c in range(chips):
        copies.append(pltpu.make_async_copy(keys, out.at[c, :tok, :], sems.at[2 * c]))
        copies.append(pltpu.make_async_copy(values, out.at[c, tok:, :], sems.at[2 * c + 1]))
    for copy in copies:
        copy.start()
    for copy in copies:
        copy.wait()


def project_kernel(d_y, w_out, out, y_held, w_held, sems):
    width = y_held.shape[2]
    copies = []
    for i in range(PARTS):
        cols = slice(i * width, (i + 1) * width)
        copies.append(
            (
                pltpu.make_async_copy(d_y.at[:, cols], y_held.at[i], sems.at[2 * i]),
                pltpu.make_async_copy(w_out.at[:, cols], w_held.at[i], sems.at[2 * i + 1]),
            )
        )
    for pair in copies:
        for copy in pair:
            copy.start()
    total = jnp.zeros(out.shape, f32)
    for i, pair in enumerate(copies):
        for copy in pair:
            copy.wait()
        total += lax.dot_general(y_held[i], w_held[i], NT, preferred_element_type=f32)
    out[...] = total.astype(bf16)


def forward_kernel(kb, bc, q_own, q_sib, kv, out, qs, qt, acc, lst, sems):
    chip, core = my_chip(), lax.axis_index("core")
    copies = head_copies(qs, q_own, q_sib, sems)
    for copy in copies:
        copy.start()
    for copy in copies:
        copy.wait()

    def per_block(j, _):
        b = query_block(j, chip, core)
        qt[...] = qs[j].T
        acc[...] = jnp.zeros_like(acc)

        def visit(carry, idxs, limits):
            m, l, l_b = carry
            k = rows_of(kv, idxs)
            v = rows_of(kv, [i + 2 for i in idxs])
            s = jnp.dot(k, qt[...], preferred_element_type=f32) * (SCALE * LOG2E)
            if limits is not None:
                s = hide(s, limits, NEG)
            m_new = jnp.maximum(m, jnp.max(s, axis=0, keepdims=True))
            alpha = jnp.exp2(m - m_new)
            p = jnp.exp2(s - m_new)
            p_b = p.astype(bf16)
            o = lax.dot_general(v, p_b, TN, preferred_element_type=f32)
            acc[...] = acc[...] * alpha + o
            return (
                m_new,
                l * alpha + jnp.sum(p, axis=0, keepdims=True),
                l_b * alpha + jnp.sum(p_b.astype(f32), axis=0, keepdims=True),
            )

        zero = jnp.zeros((1, ROWS), f32)
        m, l, l_b = walk(
            kb, bc, lst, b, core, visit, (jnp.full((1, ROWS), NEG, f32), zero, zero)
        )
        out[j, :WIDTH, :] = acc[...]
        out[j, WIDTH : WIDTH + 8, :] = jnp.concatenate(
            [m, l, l_b, jnp.zeros((5, ROWS), f32)], axis=0
        )
        return 0

    lax.fori_loop(0, 4, per_block, 0)


def backward_kernel(
    kb, bc, q_own, q_sib, g_own, g_sib, kv_in, st_own, st_sib,
    dq_own, dq_sib, dkv,
    qs, gs, qt, gt, dq, kv, acc, held, lst, sems, out_sems,
):
    chip, core = my_chip(), lax.axis_index("core")
    copies = [pltpu.make_async_copy(kv_in, kv, sems.at[4 * HEADS])]
    copies += head_copies(qs, q_own, q_sib, sems)
    for copy in copies:
        copy.start()
    stack_heads(gs, g_own, g_sib)
    acc[...] = jnp.zeros_like(acc)
    for copy in copies:
        copy.wait()

    def per_block(j, _):
        b = query_block(j, chip, core)
        peer = (j + 2) % 4
        qt[...] = qs[j].T
        gt[...] = gs[j].T
        m0, l0, n0 = (st_own[j, WIDTH + i : WIDTH + i + 1, :] for i in range(3))
        m1, l1, n1 = (st_sib[peer, WIDTH + i : WIDTH + i + 1, :] for i in range(3))
        m = jnp.maximum(m0, m1)
        a0, a1 = jnp.exp2(m0 - m), jnp.exp2(m1 - m)
        total = m + jnp.log(l0 * a0 + l1 * a1) * LOG2E
        o = st_own[j, :WIDTH, :] * a0 + st_sib[peer, :WIDTH, :] * a1
        delta = jnp.sum(o * gt[...].astype(f32), axis=0, keepdims=True) / (n0 * a0 + n1 * a1)
        dq[...] = jnp.zeros_like(dq)

        def visit(carry, idxs, limits):
            k = rows_of(kv, idxs)
            v = rows_of(kv, [i + 2 for i in idxs])
            s = jnp.dot(k, qt[...], preferred_element_type=f32) * (SCALE * LOG2E)
            p = jnp.exp2(s - total)
            if limits is not None:
                p = hide(p, limits, 0.0)
            dp = jnp.dot(v, gt[...], preferred_element_type=f32)
            ds = (p * (dp - delta)).astype(bf16)
            dk = jnp.dot(ds, qs[j], preferred_element_type=f32)
            dv = jnp.dot(p.astype(bf16), gs[j], preferred_element_type=f32)
            for t, i in enumerate(idxs):
                acc[block_rows(i), :] += dk[t * SPAN : (t + 1) * SPAN]
                acc[block_rows(i + 2), :] += dv[t * SPAN : (t + 1) * SPAN]
            dq[...] += lax.dot_general(k, ds, TN, preferred_element_type=f32)
            return carry

        walk(kb, bc, lst, b, core, visit, 0)
        row = pl.ds(pl.multiple_of((j % 2) * SPAN, SPAN), SPAN)
        for h in range(HEADS):
            piece = (dq[:, h * SPAN : (h + 1) * SPAN] * SCALE).astype(bf16).T

            @pl.when(j < 2)
            def _():
                dq_own[row, h * WIDTH : (h + 1) * WIDTH] = piece

            @pl.when(j >= 2)
            def _():
                dq_sib[row, h * WIDTH : (h + 1) * WIDTH] = piece

        return 0

    lax.fori_loop(0, 4, per_block, 0)
    half = 2 * SPAN
    copies = []
    for c in range(dkv.shape[0] // half):
        rows = slice(c * half, (c + 1) * half)
        at = 2 * c * half
        held[rows, :WIDTH] = (acc[at : at + half, :] * SCALE).astype(bf16)
        held[rows, WIDTH:] = acc[at + half : at + 2 * half, :].astype(bf16)
        copies.append(pltpu.make_async_copy(held.at[rows, :], dkv.at[rows, :], out_sems.at[c]))
        copies[-1].start()
    for copy in copies:
        copy.wait()


def per_device(queries, keys, values, d_y, w_out, key_blocks, block_count):
    chips = lax.axis_size("y") * lax.axis_size("x")
    tok = keys.shape[0]
    swap = [(0, 1), (1, 0)]
    smem = pl.BlockSpec(memory_space=pltpu.SMEM)
    vmem = pl.BlockSpec(memory_space=pltpu.VMEM)
    hbm = pl.BlockSpec(memory_space=pltpu.HBM)
    fold = [
        (2 * i + c, 2 * i if c == 0 else 2 * (chips - 1 - i) + 1)
        for i in range(chips)
        for c in range(2)
    ]
    d_y = lax.ppermute(d_y, TOKEN_AXES, fold)
    kv_sent = pl.pallas_call(
        spread_kernel,
        out_shape=jax.ShapeDtypeStruct((chips, 2 * tok, WIDTH), bf16),
        in_specs=[vmem, vmem],
        out_specs=hbm,
        scratch_shapes=[pltpu.SemaphoreType.DMA((2 * chips,))],
        cost_estimate=pl.CostEstimate(
            flops=0, bytes_accessed=chips * 2 * tok * WIDTH * 2, transcendentals=0
        ),
        name="spread_keys_values",
    )(keys, values)
    d_y, kv_sent = lax.optimization_barrier((d_y, kv_sent))
    d_y_all = lax.all_gather(d_y, "head", axis=1, tiled=True)
    kv = lax.all_to_all(kv_sent, CHIP_AXES, 0, 0).reshape(chips * 2 * tok, WIDTH)
    queries = lax.ppermute(queries, TOKEN_AXES, fold)
    q_sib = lax.ppermute(queries, "core", swap)
    queries, q_sib = (pltpu.with_memory_space_constraint(q, pltpu.HBM) for q in (queries, q_sib))

    stats = pl.pallas_call(
        forward_kernel,
        out_shape=jax.ShapeDtypeStruct((4, WIDTH + 8, ROWS), f32),
        in_specs=[smem, smem, hbm, hbm, vmem],
        out_specs=vmem,
        scratch_shapes=[
            pltpu.VMEM((4, ROWS, WIDTH), bf16),
            pltpu.VMEM((WIDTH, ROWS), bf16),
            pltpu.VMEM((WIDTH, ROWS), f32),
            pltpu.SMEM((40,), jnp.int32),
            pltpu.SemaphoreType.DMA((4 * HEADS,)),
        ],
        compiler_params=pltpu.CompilerParams(vmem_limit_bytes=48 * 2**20),
        cost_estimate=pl.CostEstimate(
            flops=6 * 10**9, bytes_accessed=4 * 2**20, transcendentals=4 * 10**6
        ),
        name="forward_statistics",
    )(key_blocks, block_count, queries, q_sib, kv)
    stats_sib = lax.ppermute(stats, "core", swap)

    att_grad = pl.pallas_call(
        project_kernel,
        out_shape=jax.ShapeDtypeStruct((tok, ROWS), bf16),
        in_specs=[hbm, hbm],
        out_specs=vmem,
        scratch_shapes=[
            pltpu.VMEM((PARTS, tok, w_out.shape[1] // PARTS), bf16),
            pltpu.VMEM((PARTS, w_out.shape[0], w_out.shape[1] // PARTS), bf16),
            pltpu.SemaphoreType.DMA((2 * PARTS,)),
        ],
        compiler_params=pltpu.CompilerParams(vmem_limit_bytes=32 * 2**20),
        cost_estimate=pl.CostEstimate(
            flops=2 * tok * w_out.size, bytes_accessed=6 * 2**20, transcendentals=0
        ),
        name="attention_cotangent",
    )(*(pltpu.with_memory_space_constraint(a, pltpu.HBM) for a in (d_y_all, w_out)))
    grad_sib = lax.ppermute(att_grad, "core", swap)

    dq_own, dq_sib, dkv = pl.pallas_call(
        backward_kernel,
        out_shape=(
            jax.ShapeDtypeStruct((tok, ROWS), bf16),
            jax.ShapeDtypeStruct((tok, ROWS), bf16),
            jax.ShapeDtypeStruct((chips * tok, 2 * WIDTH), bf16),
        ),
        in_specs=[smem, smem, hbm, hbm, vmem, vmem, hbm, vmem, vmem],
        out_specs=(vmem, vmem, hbm),
        scratch_shapes=[
            pltpu.VMEM((4, ROWS, WIDTH), bf16),
            pltpu.VMEM((4, ROWS, WIDTH), bf16),
            pltpu.VMEM((WIDTH, ROWS), bf16),
            pltpu.VMEM((WIDTH, ROWS), bf16),
            pltpu.VMEM((WIDTH, ROWS), f32),
            pltpu.VMEM((chips * 2 * tok, WIDTH), bf16),
            pltpu.VMEM((chips * 2 * tok, WIDTH), f32),
            pltpu.VMEM((chips * tok, 2 * WIDTH), bf16),
            pltpu.SMEM((40,), jnp.int32),
            pltpu.SemaphoreType.DMA((4 * HEADS + 1,)),
            pltpu.SemaphoreType.DMA((chips,)),
        ],
        compiler_params=pltpu.CompilerParams(vmem_limit_bytes=48 * 2**20),
        cost_estimate=pl.CostEstimate(
            flops=10 * 10**9, bytes_accessed=8 * 2**20, transcendentals=4 * 10**6
        ),
        name="backward_gradients",
    )(key_blocks, block_count, queries, q_sib, att_grad, grad_sib, kv, stats, stats_sib)

    d_queries = lax.ppermute(dq_own + lax.ppermute(dq_sib, "core", swap), TOKEN_AXES, fold)
    parts = lax.all_to_all(dkv.reshape(chips, tok, 2 * WIDTH), CHIP_AXES, 0, 0)
    summed = jnp.sum(parts.astype(f32), axis=0).astype(bf16)
    return d_queries, summed[:, :WIDTH], summed[:, WIDTH:]


def solution(mesh):
    ctx, head = mesh.devices.shape
    side = math.isqrt(ctx // 2)
    grid = Mesh(mesh.devices.reshape(side, side, 2, head), ("y", "x", "core", "head"))
    rows = P(TOKEN_AXES, "head")
    return jax.shard_map(
        per_device,
        mesh=grid,
        in_specs=(rows, rows, rows, rows, P("head", None), P(), P()),
        out_specs=(rows, rows, rows),
        check_vma=False,
    )
```

profile of v0, /device:TPU:1, one launch (start us, length us, event | category | flops | bytes accessed | tf_op | source)
XLA Modules:
  0.0 128.3 jit_solution(2483762066411638788)
XLA Ops:
  7.2 0.0 all-gather.2.cloned.1.call-start
  7.2 7.7 %collective-permute-start.2 = (bf16[256,512]{1,0:T(8,128)(2,1)}, bf16[256,512]{1,0:T(8,128)(2,1)S(1)}, u32[]{:S(2)}, u32[]{:S(2)}) collective-permute-start(bf16[256,512]{1,0:T(8,128)(2,1)} %param.10), channel_id=1, source_target_pairs={{0,0},{8,248},{16,16},{24,232},{32,32},{40,216},{48,48},{56,200},{... | collective-permute-start | bytes 786440 | tf_op jit(solution)/shard_map/ppermute | solution.py:287
  14.9 2.5 %spread_keys_values.1 = bf16[16,512,128]{2,1,0:T(8,128)(2,1)} custom-call(bf16[256,128]{1,0:T(8,128)(2,1)} %keys.1, bf16[256,128]{1,0:T(8,128)(2,1)} %values.1), custom_call_target="tpu_custom_call" | custom-call | bytes 2097152 | tf_op jit(solution)/shard_map/spread_keys_values/pallas_call | solution.py:288
  17.4 1.5 %collective-permute-done.2 = bf16[256,512]{1,0:T(8,128)(2,1)S(1)} collective-permute-done((bf16[256,512]{1,0:T(8,128)(2,1)}, bf16[256,512]{1,0:T(8,128)(2,1)S(1)}, u32[]{:S(2)}, u32[]{:S(2)}) %collective-permute-start.2) | collective-permute-done | bytes 262176 | tf_op jit(solution)/shard_map/ppermute | solution.py:287
  18.8 0.0 copy-start.2
  18.8 0.7 copy-done.2
  19.5 0.0 all-gather.2.cloned.1.call-update
  19.6 0.0 copy-start.4
  19.6 0.0 copy-start.3
  19.6 0.0 copy-start.1
  19.6 6.3 %all-to-all-start = ((bf16[16,512,128]{2,1,0:T(8,128)(2,1)}), bf16[16,512,128]{2,1,0:T(8,128)(2,1)S(1)}, u32[]{:S(2)}, u32[]{:S(2)}) async-start(bf16[16,512,128]{2,1,0:T(8,128)(2,1)} %spread_keys_values.1), calls=%async_computation | async-start | bytes 4194304 | tf_op jit(solution)/shard_map/all_to_all | solution.py:301
  25.9 0.0 copy-done.4
  25.9 6.6 %collective-permute-start = (bf16[256,512]{1,0:T(8,128)(2,1)S(1)}, bf16[256,512]{1,0:T(8,128)(2,1)S(1)}, u32[]{:S(2)}, u32[]{:S(2)}) collective-permute-start(bf16[256,512]{1,0:T(8,128)(2,1)S(1)} %copy-done.4), channel_id=1, source_target_pairs={{0,0},{8,248},{16,16},{24,232},{32,32},{40,216},{48,48},{56,200},{... | collective-permute-start | bytes 786440 | tf_op jit(solution)/shard_map/ppermute | solution.py:302
  32.5 19.8 %collective-permute-done.q_own = bf16[256,512]{1,0:T(8,128)(2,1)S(1)} collective-permute-done((bf16[256,512]{1,0:T(8,128)(2,1)S(1)}, bf16[256,512]{1,0:T(8,128)(2,1)S(1)}, u32[]{:S(2)}, u32[]{:S(2)}) %collective-permute-start) | collective-permute-done | bytes 262176 | tf_op jit(solution)/shard_map/ppermute | solution.py:302
  52.3 0.0 copy-start.5
  52.3 0.0 collective-permute-start.1
  52.3 0.0 copy-done.3
  52.3 0.1 copy.11.kb
  52.4 1.4 %collective-permute-done.1.q_sib = bf16[256,512]{1,0:T(8,128)(2,1)S(1)} collective-permute-done((bf16[256,512]{1,0:T(8,128)(2,1)S(1)}, bf16[256,512]{1,0:T(8,128)(2,1)S(1)}, u32[]{:S(2)}, u32[]{:S(2)}) %collective-permute-start.1) | collective-permute-done | bytes 262176 | tf_op jit(solution)/shard_map/ppermute | solution.py:303
  53.9 0.0 copy-start.6
  53.9 0.0 all-to-all-done
  53.9 0.7 copy-done.6
  54.6 0.0 copy-start
  54.6 0.0 copy-done.5
  54.6 0.0 copy-done.1
  54.6 8.7 %forward_statistics.1.st_own = f32[4,136,512]{2,1,0:T(8,128)S(1)} custom-call(s32[64,32]{1,0:T(8,128)S(1)} %copy.11.kb, s32[64]{0:T(128)S(1)} %copy-done.1, bf16[256,512]{1,0:T(8,128)(2,1)} %copy-done.5, bf16[256,512]{1,0:T(8,128)(2,1)} %copy-done.6, bf16[8192,128]{1,0:T(8,128)(2,1)S(1)} %bitcast.2), custom_call_target="tpu_custom_call" | custom-call | flops 6000000000 | bytes 4194304 | tf_op jit(solution)/shard_map/forward_statistics/pallas_call | solution.py:306
  63.3 0.0 copy-done
  63.3 1.4 %collective-permute-start.4 = (f32[4,136,512]{2,1,0:T(8,128)S(1)}, f32[4,136,512]{2,1,0:T(8,128)}, u32[]{:S(2)}, u32[]{:S(2)}) collective-permute-start(f32[4,136,512]{2,1,0:T(8,128)S(1)} %forward_statistics.1.st_own), channel_id=1, source_target_pairs={{0,8},{8,0},{1,9},{9,1},{2,10},{10,2},{3,11},{11,3},{4,12},{12,4},... | collective-permute-start | bytes 3342344 | tf_op jit(solution)/shard_map/ppermute | solution.py:324
  64.7 0.0 all-gather.2.cloned.1.call-done.d_y
  64.7 3.4 %attention_cotangent.1.g_own = bf16[256,512]{1,0:T(8,128)(2,1)S(1)} custom-call(bf16[256,4096]{1,0:T(8,128)(2,1)} %all-gather.2.cloned.1.call-done.d_y, bf16[512,4096]{1,0:T(8,128)(2,1)} %w_out.1), custom_call_target="tpu_custom_call" | custom-call | flops 1073741824 | bytes 6291456 | tf_op jit(solution)/shard_map/attention_cotangent/pallas_call | solution.py:326
  68.1 0.1 collective-permute-start.3
  68.3 0.0 collective-permute-done.4.st_sib
  68.3 1.5 %collective-permute-done.3.g_sib = bf16[256,512]{1,0:T(8,128)(2,1)S(1)} collective-permute-done((bf16[256,512]{1,0:T(8,128)(2,1)S(1)}, bf16[256,512]{1,0:T(8,128)(2,1)S(1)}, u32[]{:S(2)}, u32[]{:S(2)}) %collective-permute-start.3) | collective-permute-done | bytes 262176 | tf_op jit(solution)/shard_map/ppermute | solution.py:342
  69.8 12.6 %backward_gradients.1 = (bf16[256,512]{1,0:T(8,128)(2,1)S(1)}, bf16[256,512]{1,0:T(8,128)(2,1)S(1)}, bf16[4096,256]{1,0:T(8,128)(2,1)}) custom-call(s32[64,32]{1,0:T(8,128)S(1)} %copy.11.kb, s32[64]{0:T(128)S(1)} %copy-done.1, bf16[256,512]{1,0:T(8,128)(2,1)} %copy-done.5, bf16[256,512]{1,0:T(8,128)(2,1)} %copy-done.6, ...), custom_call_target="tpu_custom_call" | custom-call | flops 10000000000 | bytes 8388608 | tf_op jit(solution)/shard_map/backward_gradients/pallas_call | solution.py:344
  82.4 5.5 %all-to-all-start.1 = ((bf16[16,256,256]{2,1,0:T(8,128)(2,1)}), bf16[16,256,256]{2,1,0:T(8,128)(2,1)S(1)}, u32[]{:S(2)}, u32[]{:S(2)}) async-start(bf16[16,256,256]{2,1,0:T(8,128)(2,1)} %bitcast.1), calls=%async_computation.1 | async-start | bytes 4194304 | tf_op jit(solution)/shard_map/all_to_all | solution.py:374
  87.9 2.7 %collective-permute-start.5 = (bf16[256,512]{1,0:T(8,128)(2,1)S(1)}, bf16[256,512]{1,0:T(8,128)(2,1)S(1)}, u32[]{:S(2)}, u32[]{:S(2)}) collective-permute-start(bf16[256,512]{1,0:T(8,128)(2,1)S(1)} %get-tuple-element.11), channel_id=1, source_target_pairs={{0,8},{8,0},{1,9},{9,1},{2,10},{10,2},{3,11},{11,3},{4,12},{12,4},... | collective-permute-start | bytes 786440 | tf_op jit(solution)/shard_map/ppermute | solution.py:373
  90.6 1.2 collective-permute-done.5
  91.8 0.1 add.3
  91.9 6.8 %collective-permute-start.6 = (bf16[256,512]{1,0:T(8,128)(2,1)S(1)}, bf16[256,512]{1,0:T(8,128)(2,1)S(1)}, u32[]{:S(2)}, u32[]{:S(2)}) collective-permute-start(bf16[256,512]{1,0:T(8,128)(2,1)S(1)} %add.3), channel_id=1, source_target_pairs={{0,0},{8,248},{16,16},{24,232},{32,32},{40,216},{48,48},{56,200},{... | collective-permute-start | bytes 786440 | tf_op jit(solution)/shard_map/ppermute | solution.py:373
  98.7 21.1 %collective-permute-done.6 = bf16[256,512]{1,0:T(8,128)(2,1)S(1)} collective-permute-done((bf16[256,512]{1,0:T(8,128)(2,1)S(1)}, bf16[256,512]{1,0:T(8,128)(2,1)S(1)}, u32[]{:S(2)}, u32[]{:S(2)}) %collective-permute-start.6) | collective-permute-done | bytes 262176 | tf_op jit(solution)/shard_map/ppermute | solution.py:373
  119.8 0.0 all-to-all-done.1
  119.8 0.3 reduce_sum.12
  120.1 0.7 fusion
  120.7 0.7 copy.13
Async XLA Ops:
  7.2 57.6 %all-gather.2.cloned.1.call-start = ((), (), s32[]{:S(2)}) async-start(), calls=%async_computation.2 | async-start | bytes 2359296 | tf_op jit(solution)/shard_map/all_gather | solution.py:300
  7.2 11.6 %collective-permute-start.2 = (bf16[256,512]{1,0:T(8,128)(2,1)}, bf16[256,512]{1,0:T(8,128)(2,1)S(1)}, u32[]{:S(2)}, u32[]{:S(2)}) collective-permute-start(bf16[256,512]{1,0:T(8,128)(2,1)} %param.10), channel_id=1, source_target_pairs={{0,0},{8,248},{16,16},{24,232},{32,32},{40,216},{48,48},{56,200},{... | collective-permute-start | bytes 786440 | tf_op jit(solution)/shard_map/ppermute | solution.py:287
  18.8 0.7 copy-start.2
  19.6 6.3 %copy-start.4 = (bf16[256,512]{1,0:T(8,128)(2,1)S(1)}, bf16[256,512]{1,0:T(8,128)(2,1)}, u32[]{:S(2)}) copy-start(bf16[256,512]{1,0:T(8,128)(2,1)} %param.7) | copy-start | bytes 786436
  19.6 32.8 %copy-start.3 = (s32[64,32]{0,1:T(8,128)S(1)}, s32[64,32]{0,1:T(8,128)}, u32[]{:S(2)}) copy-start(s32[64,32]{0,1:T(8,128)} %param.12) | copy-start | bytes 24580
  19.6 35.0 %copy-start.1 = (s32[64]{0:T(128)S(1)}, s32[64]{0:T(128)}, u32[]{:S(2)}) copy-start(s32[64]{0:T(128)} %bc.3) | copy-start | bytes 772
  19.6 34.3 %all-to-all-start = ((bf16[16,512,128]{2,1,0:T(8,128)(2,1)}), bf16[16,512,128]{2,1,0:T(8,128)(2,1)S(1)}, u32[]{:S(2)}, u32[]{:S(2)}) async-start(bf16[16,512,128]{2,1,0:T(8,128)(2,1)} %spread_keys_values.1), calls=%async_computation | async-start | bytes 4194304 | tf_op jit(solution)/shard_map/all_to_all | solution.py:301
  25.9 26.4 %collective-permute-start = (bf16[256,512]{1,0:T(8,128)(2,1)S(1)}, bf16[256,512]{1,0:T(8,128)(2,1)S(1)}, u32[]{:S(2)}, u32[]{:S(2)}) collective-permute-start(bf16[256,512]{1,0:T(8,128)(2,1)S(1)} %copy-done.4), channel_id=1, source_target_pairs={{0,0},{8,248},{16,16},{24,232},{32,32},{40,216},{48,48},{56,200},{... | collective-permute-start | bytes 786440 | tf_op jit(solution)/shard_map/ppermute | solution.py:302
  52.3 2.3 %copy-start.5 = (bf16[256,512]{1,0:T(8,128)(2,1)}, bf16[256,512]{1,0:T(8,128)(2,1)S(1)}, u32[]{:S(2)}) copy-start(bf16[256,512]{1,0:T(8,128)(2,1)S(1)} %collective-permute-done.q_own) | copy-start | bytes 786436
  52.3 1.5 %collective-permute-start.1 = (bf16[256,512]{1,0:T(8,128)(2,1)S(1)}, bf16[256,512]{1,0:T(8,128)(2,1)S(1)}, u32[]{:S(2)}, u32[]{:S(2)}) collective-permute-start(bf16[256,512]{1,0:T(8,128)(2,1)S(1)} %collective-permute-done.q_own), channel_id=1, source_target_pairs={{0,8},{8,0},{1,9},{9,1},{2,10},{10,2},{3,11},{11,3},{4,12},{12,4},... | collective-permute-start | bytes 786440 | tf_op jit(solution)/shard_map/ppermute | solution.py:303
  53.9 0.7 copy-start.6
  54.6 8.7 %copy-start = (bf16[16,512,128]{2,1,0:T(8,128)(2,1)}, bf16[16,512,128]{2,1,0:T(8,128)(2,1)S(1)}, u32[]{:S(2)}) copy-start(bf16[16,512,128]{2,1,0:T(8,128)(2,1)S(1)} %all-to-all-done) | copy-start | bytes 6291460
  63.3 5.0 %collective-permute-start.4 = (f32[4,136,512]{2,1,0:T(8,128)S(1)}, f32[4,136,512]{2,1,0:T(8,128)}, u32[]{:S(2)}, u32[]{:S(2)}) collective-permute-start(f32[4,136,512]{2,1,0:T(8,128)S(1)} %forward_statistics.1.st_own), channel_id=1, source_target_pairs={{0,8},{8,0},{1,9},{9,1},{2,10},{10,2},{3,11},{11,3},{4,12},{12,4},... | collective-permute-start | bytes 3342344 | tf_op jit(solution)/shard_map/ppermute | solution.py:324
  68.1 1.6 %collective-permute-start.3 = (bf16[256,512]{1,0:T(8,128)(2,1)S(1)}, bf16[256,512]{1,0:T(8,128)(2,1)S(1)}, u32[]{:S(2)}, u32[]{:S(2)}) collective-permute-start(bf16[256,512]{1,0:T(8,128)(2,1)S(1)} %attention_cotangent.1.g_own), channel_id=1, source_target_pairs={{0,8},{8,0},{1,9},{9,1},{2,10},{10,2},{3,11},{11,3},{4,12},{12,4},... | collective-permute-start | bytes 786440 | tf_op jit(solution)/shard_map/ppermute | solution.py:342
  82.4 37.4 %all-to-all-start.1 = ((bf16[16,256,256]{2,1,0:T(8,128)(2,1)}), bf16[16,256,256]{2,1,0:T(8,128)(2,1)S(1)}, u32[]{:S(2)}, u32[]{:S(2)}) async-start(bf16[16,256,256]{2,1,0:T(8,128)(2,1)} %bitcast.1), calls=%async_computation.1 | async-start | bytes 4194304 | tf_op jit(solution)/shard_map/all_to_all | solution.py:374
  87.9 3.9 %collective-permute-start.5 = (bf16[256,512]{1,0:T(8,128)(2,1)S(1)}, bf16[256,512]{1,0:T(8,128)(2,1)S(1)}, u32[]{:S(2)}, u32[]{:S(2)}) collective-permute-start(bf16[256,512]{1,0:T(8,128)(2,1)S(1)} %get-tuple-element.11), channel_id=1, source_target_pairs={{0,8},{8,0},{1,9},{9,1},{2,10},{10,2},{3,11},{11,3},{4,12},{12,4},... | collective-permute-start | bytes 786440 | tf_op jit(solution)/shard_map/ppermute | solution.py:373
  91.9 27.9 %collective-permute-start.6 = (bf16[256,512]{1,0:T(8,128)(2,1)S(1)}, bf16[256,512]{1,0:T(8,128)(2,1)S(1)}, u32[]{:S(2)}, u32[]{:S(2)}) collective-permute-start(bf16[256,512]{1,0:T(8,128)(2,1)S(1)} %add.3), channel_id=1, source_target_pairs={{0,0},{8,248},{16,16},{24,232},{32,32},{40,216},{48,48},{56,200},{... | collective-permute-start | bytes 786440 | tf_op jit(solution)/shard_map/ppermute | solution.py:373
Sparse Core Ops, SparseCore 0:
  19.7 39.2 all-gather.1
where the time goes:
time: 130 us; the launch traced here: 128 us
  waiting for transfers between devices  46.5 us (36%)
  starting transfers between devices  37.2 us (29%)
  Pallas kernels  27.2 us (21%)
  between operations  14.2 us (11%)
  local copies, waits for them, and re-layouts  2.87 us (2%)
    ppermute x1, waiting for transfers between devices, per_device(): lax.ppermute(dq_own + lax.ppermute(dq_sib, 'core', swap), TOKEN_AXES, fold)  21.1 us
    ppermute x1, waiting for transfers between devices, per_device(): queries = lax.ppermute(queries, TOKEN_AXES, fold)  19.8 us
    pallas_call x1, Pallas kernels, per_device(): pl.pallas_call(backward_kernel, out_shape=(jax.ShapeDtypeStruct((tok, ROW...  12.6 us
    pallas_call x1, Pallas kernels, per_device(): pl.pallas_call(forward_kernel, out_shape=jax.ShapeDtypeStruct((4, WIDTH +...  8.69 us
    ppermute x1, starting transfers between devices, per_device(): d_y = lax.ppermute(d_y, TOKEN_AXES, fold)  7.67 us
    ppermute x1, starting transfers between devices, per_device(): lax.ppermute(dq_own + lax.ppermute(dq_sib, 'core', swap), TOKEN_AXES, fold)  6.79 us
    ppermute x1, starting transfers between devices, per_device(): queries = lax.ppermute(queries, TOKEN_AXES, fold)  6.6 us
    all_to_all x1, starting transfers between devices, per_device(): lax.all_to_all(kv_sent, CHIP_AXES, 0, 0).reshape(chips * 2 * tok, WIDTH)  6.3 us
  transfers between devices with their start and end apart: 10, of which 6 were waited for; matrix products, arithmetic and copies ran while one was open for 0% of the time, Pallas kernels for 11%

commit v1 on v0

--- a/solution.py
+++ b/solution.py
@@ -270,6 +270,20 @@
         copies[-1].start()
     for copy in copies:
         copy.wait()
+
+
+def finish_kernel(parts, dq, dq_out, keys_out, values_out, sem):
+    copy = pltpu.make_async_copy(dq, dq_out, sem)
+    copy.start()
+    rows = 64
+    for r in range(0, keys_out.shape[0], rows):
+        at = slice(r, r + rows)
+        total = parts[0, at, :].astype(f32)
+        for c in range(1, parts.shape[0]):
+            total += parts[c, at, :].astype(f32)
+        keys_out[at, :] = total[:, :WIDTH].astype(bf16)
+        values_out[at, :] = total[:, WIDTH:].astype(bf16)
+    copy.wait()
 
 
 def per_device(queries, keys, values, d_y, w_out, key_blocks, block_count):
@@ -372,8 +386,22 @@
 
     d_queries = lax.ppermute(dq_own + lax.ppermute(dq_sib, "core", swap), TOKEN_AXES, fold)
     parts = lax.all_to_all(dkv.reshape(chips, tok, 2 * WIDTH), CHIP_AXES, 0, 0)
-    summed = jnp.sum(parts.astype(f32), axis=0).astype(bf16)
-    return d_queries, summed[:, :WIDTH], summed[:, WIDTH:]
+    return pl.pallas_call(
+        finish_kernel,
+        out_shape=(
+            jax.ShapeDtypeStruct((tok, ROWS), bf16),
+            jax.ShapeDtypeStruct((tok, WIDTH), bf16),
+            jax.ShapeDtypeStruct((tok, WIDTH), bf16),
+        ),
+        in_specs=[vmem, vmem],
+        out_specs=(hbm, vmem, vmem),
+        scratch_shapes=[pltpu.SemaphoreType.DMA(())],
+        compiler_params=pltpu.CompilerParams(vmem_limit_bytes=16 * 2**20),
+        cost_estimate=pl.CostEstimate(
+            flops=chips * tok * 2 * WIDTH, bytes_accessed=3 * 2**20, transcendentals=0
+        ),
+        name="sum_partial_gradients",
+    )(parts, d_queries)
 
 
 def solution(mesh):

time: 130 us -> 133 us (1.023)
  Pallas kernels: 27.2 us -> 30.8 us
    pallas_call x1, Pallas kernels: 12.6 us -> 14.6 us  [per_device(): pl.pallas_call(backward_kernel, out_shape=(jax.ShapeDtypeStruct((tok, ROW...]
    unnamed x16 -> x21, local copies, waits for them, and re-layouts: 2.21 us -> 3.57 us
    pallas_call x0 -> x1, Pallas kernels: none -> 1.36 us  [per_device(): pl.pallas_call(finish_kernel, out_shape=(jax.ShapeDtypeStruct((tok, ROWS)...]
where the time goes in v1:
time: 133 us; the launch traced here: 132 us
  waiting for transfers between devices  46.6 us (35%)
  starting transfers between devices  36.7 us (28%)
  Pallas kernels  30.8 us (23%)
  between operations  14.2 us (11%)
  local copies, waits for them, and re-layouts  3.57 us (3%)
    ppermute x1, waiting for transfers between devices, per_device(): lax.ppermute(dq_own + lax.ppermute(dq_sib, 'core', swap), TOKEN_AXES, fold)  21.2 us
    ppermute x1, waiting for transfers between devices, per_device(): queries = lax.ppermute(queries, TOKEN_AXES, fold)  19.8 us
    pallas_call x1, Pallas kernels, per_device(): pl.pallas_call(backward_kernel, out_shape=(jax.ShapeDtypeStruct((tok, ROW...  14.6 us
    pallas_call x1, Pallas kernels, per_device(): pl.pallas_call(forward_kernel, out_shape=jax.ShapeDtypeStruct((4, WIDTH +...  8.94 us
    ppermute x1, starting transfers between devices, per_device(): d_y = lax.ppermute(d_y, TOKEN_AXES, fold)  7.67 us
    ppermute x1, starting transfers between devices, per_device(): lax.ppermute(dq_own + lax.ppermute(dq_sib, 'core', swap), TOKEN_AXES, fold)  6.88 us
    ppermute x1, starting transfers between devices, per_device(): queries = lax.ppermute(queries, TOKEN_AXES, fold)  6.6 us
    all_to_all x1, starting transfers between devices, per_device(): lax.all_to_all(kv_sent, CHIP_AXES, 0, 0).reshape(chips * 2 * tok, WIDTH)  6.3 us
  transfers between devices with their start and end apart: 10, of which 6 were waited for; matrix products, arithmetic and copies ran while one was open for 0% of the time, Pallas kernels for 11%

profile of v1, /device:TPU:1, one launch (start us, length us, event | category | flops | bytes accessed | tf_op | source)
XLA Modules:
  0.0 131.8 jit_solution(695836284757870128)
XLA Ops:
  7.2 0.0 all-gather.2.cloned.1.call-start
  7.2 7.7 %collective-permute-start.2 = (bf16[256,512]{1,0:T(8,128)(2,1)}, bf16[256,512]{1,0:T(8,128)(2,1)S(1)}, u32[]{:S(2)}, u32[]{:S(2)}) collective-permute-start(bf16[256,512]{1,0:T(8,128)(2,1)} %param.10), channel_id=1, source_target_pairs={{0,0},{8,248},{16,16},{24,232},{32,32},{40,216},{48,48},{56,200},{... | collective-permute-start | bytes 786440 | tf_op jit(solution)/shard_map/ppermute | solution.py:301
  14.9 2.5 %spread_keys_values.1 = bf16[16,512,128]{2,1,0:T(8,128)(2,1)} custom-call(bf16[256,128]{1,0:T(8,128)(2,1)} %keys.1, bf16[256,128]{1,0:T(8,128)(2,1)} %values.1), custom_call_target="tpu_custom_call" | custom-call | bytes 2097152 | tf_op jit(solution)/shard_map/spread_keys_values/pallas_call | solution.py:302
  17.4 1.5 %collective-permute-done.2 = bf16[256,512]{1,0:T(8,128)(2,1)S(1)} collective-permute-done((bf16[256,512]{1,0:T(8,128)(2,1)}, bf16[256,512]{1,0:T(8,128)(2,1)S(1)}, u32[]{:S(2)}, u32[]{:S(2)}) %collective-permute-start.2) | collective-permute-done | bytes 262176 | tf_op jit(solution)/shard_map/ppermute | solution.py:301
  18.8 0.0 copy-start.5
  18.8 0.7 copy-done.5
  19.5 0.0 all-gather.2.cloned.1.call-update
  19.6 0.0 copy-start.7
  19.6 0.0 copy-start.6
  19.6 0.0 copy-start.4
  19.6 6.3 %all-to-all-start = ((bf16[16,512,128]{2,1,0:T(8,128)(2,1)}), bf16[16,512,128]{2,1,0:T(8,128)(2,1)S(1)}, u32[]{:S(2)}, u32[]{:S(2)}) async-start(bf16[16,512,128]{2,1,0:T(8,128)(2,1)} %spread_keys_values.1), calls=%async_computation | async-start | bytes 4194304 | tf_op jit(solution)/shard_map/all_to_all | solution.py:315
  25.9 0.0 copy-done.7
  25.9 6.6 %collective-permute-start = (bf16[256,512]{1,0:T(8,128)(2,1)S(1)}, bf16[256,512]{1,0:T(8,128)(2,1)S(1)}, u32[]{:S(2)}, u32[]{:S(2)}) collective-permute-start(bf16[256,512]{1,0:T(8,128)(2,1)S(1)} %copy-done.7), channel_id=1, source_target_pairs={{0,0},{8,248},{16,16},{24,232},{32,32},{40,216},{48,48},{56,200},{... | collective-permute-start | bytes 786440 | tf_op jit(solution)/shard_map/ppermute | solution.py:316
  32.5 19.8 %collective-permute-done.q_own = bf16[256,512]{1,0:T(8,128)(2,1)S(1)} collective-permute-done((bf16[256,512]{1,0:T(8,128)(2,1)S(1)}, bf16[256,512]{1,0:T(8,128)(2,1)S(1)}, u32[]{:S(2)}, u32[]{:S(2)}) %collective-permute-start) | collective-permute-done | bytes 262176 | tf_op jit(solution)/shard_map/ppermute | solution.py:316
  52.3 0.0 copy-start.8
  52.4 0.0 collective-permute-start.1
  52.4 0.0 copy-done.6
  52.4 0.1 copy.11.kb
  52.4 1.4 %collective-permute-done.1.q_sib = bf16[256,512]{1,0:T(8,128)(2,1)S(1)} collective-permute-done((bf16[256,512]{1,0:T(8,128)(2,1)S(1)}, bf16[256,512]{1,0:T(8,128)(2,1)S(1)}, u32[]{:S(2)}, u32[]{:S(2)}) %collective-permute-start.1) | collective-permute-done | bytes 262176 | tf_op jit(solution)/shard_map/ppermute | solution.py:317
  53.9 0.0 copy-start.9
  53.9 0.0 all-to-all-done
  53.9 0.7 copy-done.9
  54.6 0.0 copy-start
  54.6 0.0 copy-done.8
  54.6 0.0 copy-done.4
  54.6 8.9 %forward_statistics.1.st_own = f32[4,136,512]{2,1,0:T(8,128)S(1)} custom-call(s32[64,32]{1,0:T(8,128)S(1)} %copy.11.kb, s32[64]{0:T(128)S(1)} %copy-done.4, bf16[256,512]{1,0:T(8,128)(2,1)} %copy-done.8, bf16[256,512]{1,0:T(8,128)(2,1)} %copy-done.9, bf16[8192,128]{1,0:T(8,128)(2,1)S(1)} %bitcast.2), custom_call_target="tpu_custom_call" | custom-call | flops 6000000000 | bytes 4194304 | tf_op jit(solution)/shard_map/forward_statistics/pallas_call | solution.py:320
  63.6 0.0 copy-done
  63.6 0.5 collective-permute-start.4
  64.1 0.0 all-gather.2.cloned.1.call-done.d_y
  64.1 3.4 %attention_cotangent.1.g_own = bf16[256,512]{1,0:T(8,128)(2,1)S(1)} custom-call(bf16[256,4096]{1,0:T(8,128)(2,1)} %all-gather.2.cloned.1.call-done.d_y, bf16[512,4096]{1,0:T(8,128)(2,1)} %w_out.1), custom_call_target="tpu_custom_call" | custom-call | flops 1073741824 | bytes 6291456 | tf_op jit(solution)/shard_map/attention_cotangent/pallas_call | solution.py:340
  67.5 0.2 collective-permute-start.3
  67.7 0.0 collective-permute-done.4.st_sib
  67.7 1.4 %collective-permute-done.3.g_sib = bf16[256,512]{1,0:T(8,128)(2,1)S(1)} collective-permute-done((bf16[256,512]{1,0:T(8,128)(2,1)S(1)}, bf16[256,512]{1,0:T(8,128)(2,1)S(1)}, u32[]{:S(2)}, u32[]{:S(2)}) %collective-permute-start.3) | collective-permute-done | bytes 262176 | tf_op jit(solution)/shard_map/ppermute | solution.py:356
  69.1 14.6 %backward_gradients.1 = (bf16[256,512]{1,0:T(8,128)(2,1)S(1)}, bf16[256,512]{1,0:T(8,128)(2,1)S(1)}, bf16[4096,256]{1,0:T(8,128)(2,1)S(1)}) custom-call(s32[64,32]{1,0:T(8,128)S(1)} %copy.11.kb, s32[64]{0:T(128)S(1)} %copy-done.4, bf16[256,512]{1,0:T(8,128)(2,1)} %copy-done.8, bf16[256,512]{1,0:T(8,128)(2,1)} %copy-done.9, ...), custom_call_target="tpu_custom_call" | custom-call | flops 10000000000 | bytes 8388608 | tf_op jit(solution)/shard_map/backward_gradients/pallas_call | solution.py:358
  83.7 0.0 copy-start.1
  83.8 1.3 %copy-done.1 = bf16[4096,256]{1,0:T(8,128)(2,1)} copy-done((bf16[4096,256]{1,0:T(8,128)(2,1)}, bf16[4096,256]{1,0:T(8,128)(2,1)S(1)}, u32[]{:S(2)}) %copy-start.1) | copy-done | bytes 2097176
  85.1 0.0 copy-start.2
  85.1 0.7 copy-done.2
  85.8 0.0 copy-start.3
  85.8 5.9 %all-to-all-start.1 = ((bf16[16,256,256]{2,1,0:T(8,128)(2,1)}), bf16[16,256,256]{2,1,0:T(8,128)(2,1)S(1)}, u32[]{:S(2)}, u32[]{:S(2)}) async-start(bf16[16,256,256]{2,1,0:T(8,128)(2,1)} %bitcast.4), calls=%async_computation.1 | async-start | bytes 4194304 | tf_op jit(solution)/shard_map/all_to_all | solution.py:388
  91.7 0.0 copy-done.3
  91.7 2.6 %collective-permute-start.5 = (bf16[256,512]{1,0:T(8,128)(2,1)S(1)}, bf16[256,512]{1,0:T(8,128)(2,1)S(1)}, u32[]{:S(2)}, u32[]{:S(2)}) collective-permute-start(bf16[256,512]{1,0:T(8,128)(2,1)S(1)} %copy-done.3), channel_id=1, source_target_pairs={{0,8},{8,0},{1,9},{9,1},{2,10},{10,2},{3,11},{11,3},{4,12},{12,4},... | collective-permute-start | bytes 786440 | tf_op jit(solution)/shard_map/ppermute | solution.py:387
  94.3 1.2 collective-permute-done.5
  95.5 0.1 add.3
  95.5 6.9 %collective-permute-start.6 = (bf16[256,512]{1,0:T(8,128)(2,1)S(1)}, bf16[256,512]{1,0:T(8,128)(2,1)S(1)}, u32[]{:S(2)}, u32[]{:S(2)}) collective-permute-start(bf16[256,512]{1,0:T(8,128)(2,1)S(1)} %add.3), channel_id=1, source_target_pairs={{0,0},{8,248},{16,16},{24,232},{32,32},{40,216},{48,48},{56,200},{... | collective-permute-start | bytes 786440 | tf_op jit(solution)/shard_map/ppermute | solution.py:387
  102.4 21.2 %collective-permute-done.6.dq = bf16[256,512]{1,0:T(8,128)(2,1)S(1)} collective-permute-done((bf16[256,512]{1,0:T(8,128)(2,1)S(1)}, bf16[256,512]{1,0:T(8,128)(2,1)S(1)}, u32[]{:S(2)}, u32[]{:S(2)}) %collective-permute-start.6) | collective-permute-done | bytes 262176 | tf_op jit(solution)/shard_map/ppermute | solution.py:387
  123.6 0.0 all-to-all-done.1.parts
  123.6 1.4 %sum_partial_gradients.1 = (bf16[256,512]{1,0:T(8,128)(2,1)}, bf16[256,128]{1,0:T(8,128)(2,1)}, bf16[256,128]{1,0:T(8,128)(2,1)}) custom-call(bf16[16,256,256]{2,1,0:T(8,128)(2,1)S(1)} %all-to-all-done.1.parts, bf16[256,512]{1,0:T(8,128)(2,1)S(1)} %collective-permute-done.6.dq), custom_call_target="tpu_custom_call" | custom-call | flops 1048576 | bytes 3145728 | tf_op jit(solution)/shard_map/sum_partial_gradients/pallas_call | solution.py:389
Async XLA Ops:
  7.2 56.9 %all-gather.2.cloned.1.call-start = ((), (), s32[]{:S(2)}) async-start(), calls=%async_computation.2 | async-start | bytes 2359296 | tf_op jit(solution)/shard_map/all_gather | solution.py:314
  7.2 11.6 %collective-permute-start.2 = (bf16[256,512]{1,0:T(8,128)(2,1)}, bf16[256,512]{1,0:T(8,128)(2,1)S(1)}, u32[]{:S(2)}, u32[]{:S(2)}) collective-permute-start(bf16[256,512]{1,0:T(8,128)(2,1)} %param.10), channel_id=1, source_target_pairs={{0,0},{8,248},{16,16},{24,232},{32,32},{40,216},{48,48},{56,200},{... | collective-permute-start | bytes 786440 | tf_op jit(solution)/shard_map/ppermute | solution.py:301
  18.8 0.7 copy-start.5
  19.6 6.3 %copy-start.7 = (bf16[256,512]{1,0:T(8,128)(2,1)S(1)}, bf16[256,512]{1,0:T(8,128)(2,1)}, u32[]{:S(2)}) copy-start(bf16[256,512]{1,0:T(8,128)(2,1)} %param.7) | copy-start | bytes 786436
  19.6 32.8 %copy-start.6 = (s32[64,32]{0,1:T(8,128)S(1)}, s32[64,32]{0,1:T(8,128)}, u32[]{:S(2)}) copy-start(s32[64,32]{0,1:T(8,128)} %param.12) | copy-start | bytes 24580
  19.6 35.0 %copy-start.4 = (s32[64]{0:T(128)S(1)}, s32[64]{0:T(128)}, u32[]{:S(2)}) copy-start(s32[64]{0:T(128)} %bc.3) | copy-start | bytes 772
  19.6 34.3 %all-to-all-start = ((bf16[16,512,128]{2,1,0:T(8,128)(2,1)}), bf16[16,512,128]{2,1,0:T(8,128)(2,1)S(1)}, u32[]{:S(2)}, u32[]{:S(2)}) async-start(bf16[16,512,128]{2,1,0:T(8,128)(2,1)} %spread_keys_values.1), calls=%async_computation | async-start | bytes 4194304 | tf_op jit(solution)/shard_map/all_to_all | solution.py:315
  25.9 26.4 %collective-permute-start = (bf16[256,512]{1,0:T(8,128)(2,1)S(1)}, bf16[256,512]{1,0:T(8,128)(2,1)S(1)}, u32[]{:S(2)}, u32[]{:S(2)}) collective-permute-start(bf16[256,512]{1,0:T(8,128)(2,1)S(1)} %copy-done.7), channel_id=1, source_target_pairs={{0,0},{8,248},{16,16},{24,232},{32,32},{40,216},{48,48},{56,200},{... | collective-permute-start | bytes 786440 | tf_op jit(solution)/shard_map/ppermute | solution.py:316
  52.3 2.3 %copy-start.8 = (bf16[256,512]{1,0:T(8,128)(2,1)}, bf16[256,512]{1,0:T(8,128)(2,1)S(1)}, u32[]{:S(2)}) copy-start(bf16[256,512]{1,0:T(8,128)(2,1)S(1)} %collective-permute-done.q_own) | copy-start | bytes 786436
  52.4 1.5 %collective-permute-start.1 = (bf16[256,512]{1,0:T(8,128)(2,1)S(1)}, bf16[256,512]{1,0:T(8,128)(2,1)S(1)}, u32[]{:S(2)}, u32[]{:S(2)}) collective-permute-start(bf16[256,512]{1,0:T(8,128)(2,1)S(1)} %collective-permute-done.q_own), channel_id=1, source_target_pairs={{0,8},{8,0},{1,9},{9,1},{2,10},{10,2},{3,11},{11,3},{4,12},{12,4},... | collective-permute-start | bytes 786440 | tf_op jit(solution)/shard_map/ppermute | solution.py:317
  53.9 0.7 copy-start.9
  54.6 9.0 %copy-start = (bf16[16,512,128]{2,1,0:T(8,128)(2,1)}, bf16[16,512,128]{2,1,0:T(8,128)(2,1)S(1)}, u32[]{:S(2)}) copy-start(bf16[16,512,128]{2,1,0:T(8,128)(2,1)S(1)} %all-to-all-done) | copy-start | bytes 6291460
  63.6 4.1 %collective-permute-start.4 = (f32[4,136,512]{2,1,0:T(8,128)S(1)}, f32[4,136,512]{2,1,0:T(8,128)}, u32[]{:S(2)}, u32[]{:S(2)}) collective-permute-start(f32[4,136,512]{2,1,0:T(8,128)S(1)} %forward_statistics.1.st_own), channel_id=1, source_target_pairs={{0,8},{8,0},{1,9},{9,1},{2,10},{10,2},{3,11},{11,3},{4,12},{12,4},... | collective-permute-start | bytes 3342344 | tf_op jit(solution)/shard_map/ppermute | solution.py:338
  67.5 1.6 %collective-permute-start.3 = (bf16[256,512]{1,0:T(8,128)(2,1)S(1)}, bf16[256,512]{1,0:T(8,128)(2,1)S(1)}, u32[]{:S(2)}, u32[]{:S(2)}) collective-permute-start(bf16[256,512]{1,0:T(8,128)(2,1)S(1)} %attention_cotangent.1.g_own), channel_id=1, source_target_pairs={{0,8},{8,0},{1,9},{9,1},{2,10},{10,2},{3,11},{11,3},{4,12},{12,4},... | collective-permute-start | bytes 786440 | tf_op jit(solution)/shard_map/ppermute | solution.py:356
  83.7 1.3 %copy-start.1 = (bf16[4096,256]{1,0:T(8,128)(2,1)}, bf16[4096,256]{1,0:T(8,128)(2,1)S(1)}, u32[]{:S(2)}) copy-start(bf16[4096,256]{1,0:T(8,128)(2,1)S(1)} %get-tuple-element.10) | copy-start | bytes 6291460
  85.1 0.7 copy-start.2
  85.8 5.9 %copy-start.3 = (bf16[256,512]{1,0:T(8,128)(2,1)S(1)}, bf16[256,512]{1,0:T(8,128)(2,1)}, u32[]{:S(2)}) copy-start(bf16[256,512]{1,0:T(8,128)(2,1)} %copy-done.2) | copy-start | bytes 786436
  85.8 37.8 %all-to-all-start.1 = ((bf16[16,256,256]{2,1,0:T(8,128)(2,1)}), bf16[16,256,256]{2,1,0:T(8,128)(2,1)S(1)}, u32[]{:S(2)}, u32[]{:S(2)}) async-start(bf16[16,256,256]{2,1,0:T(8,128)(2,1)} %bitcast.4), calls=%async_computation.1 | async-start | bytes 4194304 | tf_op jit(solution)/shard_map/all_to_all | solution.py:388
  91.7 3.8 %collective-permute-start.5 = (bf16[256,512]{1,0:T(8,128)(2,1)S(1)}, bf16[256,512]{1,0:T(8,128)(2,1)S(1)}, u32[]{:S(2)}, u32[]{:S(2)}) collective-permute-start(bf16[256,512]{1,0:T(8,128)(2,1)S(1)} %copy-done.3), channel_id=1, source_target_pairs={{0,8},{8,0},{1,9},{9,1},{2,10},{10,2},{3,11},{11,3},{4,12},{12,4},... | collective-permute-start | bytes 786440 | tf_op jit(solution)/shard_map/ppermute | solution.py:387
  95.5 28.1 %collective-permute-start.6 = (bf16[256,512]{1,0:T(8,128)(2,1)S(1)}, bf16[256,512]{1,0:T(8,128)(2,1)S(1)}, u32[]{:S(2)}, u32[]{:S(2)}) collective-permute-start(bf16[256,512]{1,0:T(8,128)(2,1)S(1)} %add.3), channel_id=1, source_target_pairs={{0,0},{8,248},{16,16},{24,232},{32,32},{40,216},{48,48},{56,200},{... | collective-permute-start | bytes 786440 | tf_op jit(solution)/shard_map/ppermute | solution.py:387
Sparse Core Ops, SparseCore 0:
  19.7 39.2 all-gather.1
